TPU v7x, 32 devices: a whole 2x2x4 slice. The times are simulated.
32 devices in a mesh: gx: 2 (over x), gy: 4 (over z), gz: 4 (over y, core).
Axes of the slice: x: 2, y: 2, z: 4, core: 2. Of those that a mesh axis runs over, the one named last changes fastest.
Arguments:
- volume: float32 [16, 8, 64, 512], P(None, 'gx', 'gy', 'gz'), may hold values from -26 to 26
- weight: float32 [16, 16, 3, 3, 3], replicated, may hold values from -0.3125 to 0.3125
- gamma: float32 [16], replicated, may hold values from 0.5 to 1.5
- beta: float32 [16], replicated, may hold values from -0.5 to 0.5
- cotangent: float32 [16, 8, 64, 512], P(None, 'gx', 'gy', 'gz'), may hold values from -6 to 6
Outputs:
- input_grad: float32 [16, 8, 64, 512], P(None, 'gx', 'gy', 'gz')
- weight_grad: float32 [16, 16, 3, 3, 3], replicated
- gamma_grad: float32 [16], replicated
- beta_grad: float32 [16], replicated
All inputs are finite; a program needn't handle non-finite values.
Results may differ from a plain program's by a relative error of at most 0.0003.
Values sent between devices are 32-bit elements; how exact they have to be, the bound alone decides.
No kernel may reach another device: no remote copies, remote signals or barrier semaphores. Data moves between devices by JAX's collectives and lax.ppermute only.
A program may use at most 64 MiB of HBM per device.

v0:
```python
import jax
import jax.numpy as jnp
from jax import lax
from jax.sharding import PartitionSpec as P


def with_halo(block, sides, width):
    for axis, dim in sides:
        count = lax.axis_size(axis)
        forward = [(i, i + 1) for i in range(count - 1)]
        forward.append((count - 1, 0))
        backward = [(target, source) for source, target in forward]
        low = lax.ppermute(
            lax.slice_in_dim(block, block.shape[dim] - width, None, axis=dim), axis, forward
        )
        high = lax.ppermute(lax.slice_in_dim(block, 0, width, axis=dim), axis, backward)
        block = jnp.concatenate([low, block, high], axis=dim)
    return block


def mix(kernel, slab):
    return jnp.einsum("oi,ixyz->oxyz", kernel, slab, precision=lax.Precision.HIGHEST)


def contract(left, slab):
    return jnp.einsum("oxyz,ixyz->oi", left, slab, precision=lax.Precision.HIGHEST)


def shards(volume, weight, gamma, beta, cotangent):
    chans, cells_x, cells_y, cells_z = volume.shape
    count = float(
        cells_x
        * cells_y
        * cells_z
        * lax.axis_size("gx")
        * lax.axis_size("gy")
        * lax.axis_size("gz")
    )
    padded = with_halo(volume, (("gx", 1), ("gy", 2), ("gz", 3)), 1)

    def window(source, first, second, third):
        return source[
            :, first : first + cells_x, second : second + cells_y, third : third + cells_z
        ]

    conv = jnp.zeros(volume.shape, jnp.float32)
    for first in range(3):
        for second in range(3):
            for third in range(3):
                conv = conv + mix(
                    weight[:, :, first, second, third], window(padded, first, second, third)
                )
    first_sum, square_sum = lax.psum(
        (jnp.sum(conv, axis=(1, 2, 3)), jnp.sum(conv * conv, axis=(1, 2, 3))), ("gx", "gy", "gz")
    )
    mean = first_sum / count
    var = square_sum / count - mean * mean
    centred = conv - mean[:, None, None, None]
    rstd = lax.rsqrt(var + 1e-05)
    normed = centred * rstd[:, None, None, None]
    act = gamma[:, None, None, None] * normed + beta[:, None, None, None]
    sig = jax.nn.sigmoid(act)
    act_grad = cotangent * sig * (1.0 + act * (1.0 - sig))
    scale = gamma * rstd
    gamma_grad, beta_grad = lax.psum(
        (jnp.sum(act_grad * normed, axis=(1, 2, 3)), jnp.sum(act_grad, axis=(1, 2, 3))),
        ("gx", "gy", "gz"),
    )
    conv_grad = scale[:, None, None, None] * (
        act_grad
        - (beta_grad / count)[:, None, None, None]
        - normed * (gamma_grad / count)[:, None, None, None]
    )
    pieces = []
    for first in range(3):
        for second in range(3):
            for third in range(3):
                pieces.append(contract(conv_grad, window(padded, first, second, third)))
    weight_grad = lax.psum(
        jnp.stack(pieces, axis=2).reshape(chans, chans, 3, 3, 3), ("gx", "gy", "gz")
    )
    grad_padded = with_halo(conv_grad, (("gx", 1), ("gy", 2), ("gz", 3)), 1)
    input_grad = jnp.zeros(volume.shape, jnp.float32)
    for first in range(3):
        for second in range(3):
            for third in range(3):
                input_grad = input_grad + mix(
                    weight[:, :, first, second, third].T,
                    window(grad_padded, 2 - first, 2 - second, 2 - third),
                )
    return (input_grad, weight_grad, gamma_grad, beta_grad)


def solution(mesh):
    return jax.shard_map(
        shards,
        mesh=mesh,
        in_specs=(P(None, "gx", "gy", "gz"), P(), P(), P(), P(None, "gx", "gy", "gz")),
        out_specs=(P(None, "gx", "gy", "gz"), P(), P(), P()),
        check_vma=False,
    )
```

profile of v0, /device:TPU:0, one launch (start us, length us, event | category | flops | bytes accessed | tf_op | source)
XLA Modules:
  0.0 250.0 jit_solution(15097560473422288166)
XLA Ops:
  0.6 1.1 fusion.319
  1.7 3.0 %collective-permute-start = (f32[16,1,16,128]{3,0,2,1:T(8,128)S(1)}, f32[16,1,16,128]{3,0,2,1:T(8,128)S(1)}, u32[]{:S(2)}, u32[]{:S(2)}) collective-permute-start(f32[16,1,16,128]{3,0,2,1:T(8,128)S(1)} %copy.207), channel_id=1, source_target_pairs={{0,16},{16,0},{1,17},{17,1},{2,18},{18,2},{3,19},{19,3},{4,20},{20... | collective-permute-start | bytes 393224 | tf_op jit(solution)/shard_map/ppermute | solution.py:13
  4.9 2.7 %fusion.206 = f32[16,4,16,128]{3,0,2,1:T(8,128)} fusion(f32[16,16,3,3,3]{1,0,4,3,2:T(8,128)} %param.6, f32[16,4,16,128]{3,2,1,0:T(8,128)} %param.5), kind=kOutput, calls=%fused_computation.290 | convolution fusion | flops 25165824 | bytes 1056768 | tf_op jit(solution)/shard_map/oi,ixyz->oxyz/dot_general | solution.py:22
  7.6 1.5 collective-permute-done
  9.5 1.6 collective-permute-done.1
  11.1 1.9 collective-permute-start.2
  13.0 2.1 collective-permute-start.3
  15.1 2.1 fusion.225
  17.2 2.1 convolution_bitcast_fusion.4
  21.0 1.9 collective-permute-start.5
  22.9 2.1 fusion.85
  25.0 2.1 fusion.86
  27.1 2.1 fusion.87
  29.1 2.1 convolution_bitcast_fusion.3
  31.2 2.1 convolution_bitcast_fusion.5
  33.3 2.1 convolution_bitcast_fusion.6
  36.1 1.6 copy.51
  37.7 1.8 maximum_maximum_fusion
  47.1 1.1 convolution_bitcast_fusion.18
  50.1 1.0 fusion.44
  51.6 1.2 fusion.312
  52.8 38.9 %all-reduce.1 = (f32[16]{0:T(128)S(1)}, f32[16]{0:T(128)S(1)}) all-reduce(f32[16]{0:T(128)S(1)} %get-tuple-element.15, f32[16]{0:T(128)S(1)} %get-tuple-element.14), channel_id=1, replica_groups=mesh['gx'=2,'gy'=4,'gz'=4] {'gx','gy','gz'}, use_global_device_ids=true, to_apply=%region_1.0 | all-reduce | flops 32 | bytes 256 | tf_op jit(solution)/shard_map/psum | solution.py:53
  91.7 2.4 fusion.311
  94.1 40.5 %all-reduce = (f32[16]{0:T(128)S(1)}, f32[16]{0:T(128)S(1)}) all-reduce(f32[16]{0:T(128)S(1)} %get-tuple-element.13, f32[16]{0:T(128)S(1)} %get-tuple-element.12), channel_id=1, replica_groups=mesh['gx'=2,'gy'=4,'gz'=4] {'gx','gy','gz'}, use_global_device_ids=true, to_apply=%region_7.0 | all-reduce | flops 32 | bytes 256 | tf_op jit(solution)/shard_map/psum | solution.py:65
  134.6 1.4 subtract_multiply_fusion
  147.4 1.0 fusion.64
  160.2 41.9 %psum.39 = f32[16,16,3,3,3]{1,0,4,3,2:T(8,128)} all-reduce(f32[16,16,3,3,3]{1,0,4,3,2:T(8,128)} %bitcast.644), channel_id=1, replica_groups=mesh['gx'=2,'gy'=4,'gz'=4] {'gx','gy','gz'}, use_global_device_ids=true, to_apply=%region_8.0 | all-reduce | flops 6912 | bytes 55296 | tf_op jit(solution)/shard_map/psum | solution.py:79
  202.1 1.6 collective-permute-start.6
  204.2 1.4 fusion.204
  205.6 2.5 collective-permute-done.6
  208.0 1.4 collective-permute-done.7
  209.4 2.2 collective-permute-start.9
  211.7 1.4 fusion.78
  213.7 3.9 %collective-permute-done.8 = f32[16,6,1,128]{3,0,2,1:T(8,128)S(1)} collective-permute-done((f32[16,6,1,128]{3,0,2,1:T(8,128)S(1)}, f32[16,6,1,128]{3,0,2,1:T(8,128)S(1)}, u32[]{:S(2)}, u32[]{:S(2)}) %collective-permute-start.8) | collective-permute-done | bytes 49184 | tf_op jit(solution)/shard_map/ppermute | solution.py:13
  217.6 1.2 fusion.315
  218.8 1.8 copy.56
  221.9 1.4 fusion.177
  223.3 1.4 fusion.175
  224.7 1.4 fusion.176
  226.1 1.4 fusion.174
  227.5 1.4 convolution_bitcast_fusion.2
  228.9 1.4 convolution_bitcast_fusion
  230.3 1.6 copy.57
  231.9 1.6 copy.61
  233.5 2.0 pad_maximum_fusion.3
  246.5 1.1 fusion.46
  247.8 1.0 fusion.48
  248.8 1.0 copy.88
  (158 shorter events, 49.1 us)
Async XLA Ops:
  0.6 8.5 %copy-start.2 = (f32[16,4,16,128]{3,2,1,0:T(8,128)S(1)}, f32[16,4,16,128]{3,2,1,0:T(8,128)}, u32[]{:S(2)}) copy-start(f32[16,4,16,128]{3,2,1,0:T(8,128)} %param.5) | copy-start | bytes 1572868
  1.7 7.4 %collective-permute-start = (f32[16,1,16,128]{3,0,2,1:T(8,128)S(1)}, f32[16,1,16,128]{3,0,2,1:T(8,128)S(1)}, u32[]{:S(2)}, u32[]{:S(2)}) collective-permute-start(f32[16,1,16,128]{3,0,2,1:T(8,128)S(1)} %copy.207), channel_id=1, source_target_pairs={{0,16},{16,0},{1,17},{17,1},{2,18},{18,2},{3,19},{19,3},{4,20},{20... | collective-permute-start | bytes 393224 | tf_op jit(solution)/shard_map/ppermute | solution.py:13
  4.8 6.3 %collective-permute-start.1 = (f32[16,1,16,128]{3,0,2,1:T(8,128)S(1)}, f32[16,1,16,128]{3,0,2,1:T(8,128)S(1)}, u32[]{:S(2)}, u32[]{:S(2)}) collective-permute-start(f32[16,1,16,128]{3,0,2,1:T(8,128)S(1)} %copy.208), channel_id=1, source_target_pairs={{16,0},{0,16},{17,1},{1,17},{18,2},{2,18},{19,3},{3,19},{20,4},{4,... | collective-permute-start | bytes 393224 | tf_op jit(solution)/shard_map/ppermute | solution.py:16
  9.5 9.7 %copy-start.7 = (f32[16,5,16,128]{3,0,2,1:T(8,128)}, f32[16,5,16,128]{3,0,2,1:T(8,128)S(1)}, u32[]{:S(2)}) copy-start(f32[16,5,16,128]{3,0,2,1:T(8,128)S(1)} %get-tuple-element.37) | copy-start | bytes 1966084
  11.1 8.1 %copy-start.5 = (f32[16,5,16,128]{3,0,2,1:T(8,128)}, f32[16,5,16,128]{3,0,2,1:T(8,128)S(1)}, u32[]{:S(2)}) copy-start(f32[16,5,16,128]{3,0,2,1:T(8,128)S(1)} %get-tuple-element.44) | copy-start | bytes 1966084
  11.1 8.1 %collective-permute-start.2 = (f32[16,6,1,128]{3,0,2,1:T(8,128)S(1)}, f32[16,6,1,128]{3,0,2,1:T(8,128)S(1)}, u32[]{:S(2)}, u32[]{:S(2)}) collective-permute-start(f32[16,6,1,128]{3,0,2,1:T(8,128)S(1)} %get-tuple-element.33), channel_id=1, source_target_pairs={{0,4},{4,8},{8,12},{12,0},{1,5},{5,9},{9,13},{13,1},{2,6},{6,10},{... | collective-permute-start | bytes 147464 | tf_op jit(solution)/shard_map/ppermute | solution.py:13
  13.0 6.2 %collective-permute-start.3 = (f32[16,6,1,128]{3,0,2,1:T(8,128)S(1)}, f32[16,6,1,128]{3,0,2,1:T(8,128)S(1)}, u32[]{:S(2)}, u32[]{:S(2)}) collective-permute-start(f32[16,6,1,128]{3,0,2,1:T(8,128)S(1)} %get-tuple-element.34), channel_id=1, source_target_pairs={{4,0},{8,4},{12,8},{0,12},{5,1},{9,5},{13,9},{1,13},{6,2},{10,6},{... | collective-permute-start | bytes 147464 | tf_op jit(solution)/shard_map/ppermute | solution.py:16
  20.3 15.1 %collective-permute-start.4 = (f32[16,6,18,1]{2,0,3,1:T(8,128)S(1)}, f32[16,6,18,1]{2,0,3,1:T(8,128)S(1)}, u32[]{:S(2)}, u32[]{:S(2)}) collective-permute-start(f32[16,6,18,1]{2,0,3,1:T(8,128)S(1)} %copy.48), channel_id=1, source_target_pairs={{0,1},{1,2},{2,3},{3,0},{4,5},{5,6},{6,7},{7,4},{8,9},{9,10},{10,1... | collective-permute-start | bytes 20744 | tf_op jit(solution)/shard_map/ppermute | solution.py:13
  21.0 15.1 %collective-permute-start.5 = (f32[16,6,18,1]{2,0,3,1:T(8,128)S(1)}, f32[16,6,18,1]{2,0,3,1:T(8,128)S(1)}, u32[]{:S(2)}, u32[]{:S(2)}) collective-permute-start(f32[16,6,18,1]{2,0,3,1:T(8,128)S(1)} %copy.50), channel_id=1, source_target_pairs={{1,0},{2,1},{3,2},{0,3},{5,4},{6,5},{7,6},{4,7},{9,8},{10,9},{11,1... | collective-permute-start | bytes 20744 | tf_op jit(solution)/shard_map/ppermute | solution.py:16
  37.7 1.8 copy-start.26
  39.5 11.6 %copy-start = (f32[16,6,18,129]{3,0,2,1:T(8,128)}, f32[16,6,18,129]{3,0,2,1:T(8,128)S(1)}, u32[]{:S(2)}) copy-start(f32[16,6,18,129]{3,0,2,1:T(8,128)S(1)} %get-tuple-element.28) | copy-start | bytes 2674948
  48.2 1.9 copy-start.11
  48.2 1.9 copy-start.12
  48.2 1.9 copy-start.23
  48.2 1.9 copy-start.24
  48.2 1.9 copy-start.25
  50.1 1.0 copy-start.9
  50.1 1.2 copy-start.17
  50.1 1.3 copy-start.18
  50.1 1.5 copy-start.19
  51.6 40.1 %copy-start.31 = (f32[16]{0:T(128)S(1)}, f32[16]{0:T(128)}, u32[]{:S(2)}) copy-start(f32[16]{0:T(128)} %param.7) | copy-start | bytes 196
  51.6 40.1 %copy-start.32 = (f32[16]{0:T(128)S(1)}, f32[16]{0:T(128)}, u32[]{:S(2)}) copy-start(f32[16]{0:T(128)} %param.8) | copy-start | bytes 196
  52.8 81.8 %copy-start.4 = (f32[16,4,16,128]{3,0,2,1:T(8,128)}, f32[16,4,16,128]{3,0,2,1:T(8,128)S(1)}, u32[]{:S(2)}) copy-start(f32[16,4,16,128]{3,0,2,1:T(8,128)S(1)} %get-tuple-element.47) | copy-start | bytes 1572868
  134.6 3.7 %copy-start.33 = (f32[16]{0:T(128)}, f32[16]{0:T(128)S(1)}, u32[]{:S(2)}) copy-start(f32[16]{0:T(128)S(1)} %get-tuple-element.16) | copy-start | bytes 196
  134.6 3.7 %copy-start.34 = (f32[16]{0:T(128)}, f32[16]{0:T(128)S(1)}, u32[]{:S(2)}) copy-start(f32[16]{0:T(128)S(1)} %get-tuple-element.17) | copy-start | bytes 196
  136.0 2.3 copy-start.1
  137.5 2.5 %copy-start.8 = (f32[16,5,16,128]{3,0,2,1:T(8,128)S(1)}, f32[16,5,16,128]{3,0,2,1:T(8,128)}, u32[]{:S(2)}) copy-start(f32[16,5,16,128]{3,0,2,1:T(8,128)} %copy-done.7) | copy-start | bytes 1966084
  145.0 2.5 copy-start.3
  152.6 2.5 %copy-start.6 = (f32[16,5,16,128]{3,0,2,1:T(8,128)S(1)}, f32[16,5,16,128]{3,0,2,1:T(8,128)}, u32[]{:S(2)}) copy-start(f32[16,5,16,128]{3,0,2,1:T(8,128)} %copy-done.5) | copy-start | bytes 1966084
  157.0 47.2 %copy-start.27 = (f32[16,16,3,3,3]{1,0,4,3,2:T(8,128)S(1)}, f32[16,16,3,3,3]{1,0,4,3,2:T(8,128)}, u32[]{:S(2)}) copy-start(f32[16,16,3,3,3]{1,0,4,3,2:T(8,128)} %param.6) | copy-start | bytes 82948
  157.8 44.3 %copy-start.30 = (f32[16,1,16,128]{3,0,2,1:T(8,128)S(1)}, f32[16,1,16,128]{3,0,2,1:T(8,128)}, u32[]{:S(2)}) copy-start(f32[16,1,16,128]{3,0,2,1:T(8,128)} %get-tuple-element.35) | copy-start | bytes 393220
  157.8 45.9 %copy-start.29 = (f32[16,1,16,128]{3,0,2,1:T(8,128)S(1)}, f32[16,1,16,128]{3,0,2,1:T(8,128)}, u32[]{:S(2)}) copy-start(f32[16,1,16,128]{3,0,2,1:T(8,128)} %get-tuple-element.36) | copy-start | bytes 393220
  159.5 0.7 copy-start.28
  202.1 5.9 %collective-permute-start.6 = (f32[16,1,16,128]{3,0,2,1:T(8,128)S(1)}, f32[16,1,16,128]{3,0,2,1:T(8,128)S(1)}, u32[]{:S(2)}, u32[]{:S(2)}) collective-permute-start(f32[16,1,16,128]{3,0,2,1:T(8,128)S(1)} %copy-done.30), channel_id=1, source_target_pairs={{0,16},{16,0},{1,17},{17,1},{2,18},{18,2},{3,19},{19,3},{4,20},{20... | collective-permute-start | bytes 393224 | tf_op jit(solution)/shard_map/ppermute | solution.py:13
  203.7 5.7 %collective-permute-start.7 = (f32[16,1,16,128]{3,0,2,1:T(8,128)S(1)}, f32[16,1,16,128]{3,0,2,1:T(8,128)S(1)}, u32[]{:S(2)}, u32[]{:S(2)}) collective-permute-start(f32[16,1,16,128]{3,0,2,1:T(8,128)S(1)} %copy-done.29), channel_id=1, source_target_pairs={{16,0},{0,16},{17,1},{1,17},{18,2},{2,18},{19,3},{3,19},{20,4},{4,... | collective-permute-start | bytes 393224 | tf_op jit(solution)/shard_map/ppermute | solution.py:16
  209.4 4.2 %collective-permute-start.9 = (f32[16,6,1,128]{3,0,2,1:T(8,128)S(1)}, f32[16,6,1,128]{3,0,2,1:T(8,128)S(1)}, u32[]{:S(2)}, u32[]{:S(2)}) collective-permute-start(f32[16,6,1,128]{3,0,2,1:T(8,128)S(1)} %get-tuple-element.32), channel_id=1, source_target_pairs={{4,0},{8,4},{12,8},{0,12},{5,1},{9,5},{13,9},{1,13},{6,2},{10,6},{... | collective-permute-start | bytes 147464 | tf_op jit(solution)/shard_map/ppermute | solution.py:16
  211.7 5.9 %collective-permute-start.8 = (f32[16,6,1,128]{3,0,2,1:T(8,128)S(1)}, f32[16,6,1,128]{3,0,2,1:T(8,128)S(1)}, u32[]{:S(2)}, u32[]{:S(2)}) collective-permute-start(f32[16,6,1,128]{3,0,2,1:T(8,128)S(1)} %get-tuple-element.31), channel_id=1, source_target_pairs={{0,4},{4,8},{8,12},{12,0},{1,5},{5,9},{9,13},{13,1},{2,6},{6,10},{... | collective-permute-start | bytes 147464 | tf_op jit(solution)/shard_map/ppermute | solution.py:13
  220.7 9.7 %collective-permute-start.10 = (f32[16,6,18,1]{2,0,3,1:T(8,128)S(1)}, f32[16,6,18,1]{2,0,3,1:T(8,128)S(1)}, u32[]{:S(2)}, u32[]{:S(2)}) collective-permute-start(f32[16,6,18,1]{2,0,3,1:T(8,128)S(1)} %copy.56), channel_id=1, source_target_pairs={{1,0},{2,1},{3,2},{0,3},{5,4},{6,5},{7,6},{4,7},{9,8},{10,9},{11,1... | collective-permute-start | bytes 20744 | tf_op jit(solution)/shard_map/ppermute | solution.py:16
  221.4 10.6 %collective-permute-start.11 = (f32[16,6,18,1]{2,0,3,1:T(8,128)S(1)}, f32[16,6,18,1]{2,0,3,1:T(8,128)S(1)}, u32[]{:S(2)}, u32[]{:S(2)}) collective-permute-start(f32[16,6,18,1]{2,0,3,1:T(8,128)S(1)} %copy.60), channel_id=1, source_target_pairs={{0,1},{1,2},{2,3},{3,0},{4,5},{5,6},{6,7},{7,4},{8,9},{9,10},{10,1... | collective-permute-start | bytes 20744 | tf_op jit(solution)/shard_map/ppermute | solution.py:13
  244.1 2.3 copy-start.10
  244.1 2.3 copy-start.13
  244.1 2.3 copy-start.20
  244.3 2.1 copy-start.21
  244.3 2.1 copy-start.22
  246.4 1.1 copy-start.14
  246.4 1.2 copy-start.15
  246.4 1.3 copy-start.16
where the time goes:
time: 255 us; the launch traced here: 250 us
  blocking collectives  121 us (47%)
  matrix products  78.7 us (31%)
  local copies, waits for them, and re-layouts  15.7 us (6%)
  starting transfers between devices  13.8 us (5%)
  waiting for transfers between devices  10.9 us (4%)
  other arithmetic  7.77 us (3%)
    dot_general x54, matrix products, mix(): jnp.einsum('oi,ixyz->oxyz', kernel, slab, precision=lax.Precision.HIGHEST)  56 us
    psum x1, blocking collectives, shards(): lax.psum(jnp.stack(pieces, axis=2).reshape(chans, chans, 3, 3, 3), ('gx',...  41.9 us
    psum x1, blocking collectives, shards(): lax.psum((jnp.sum(act_grad * normed, axis=(1, 2, 3)), jnp.sum(act_grad, a...  40.5 us
    psum x1, blocking collectives, shards(): lax.psum((jnp.sum(conv, axis=(1, 2, 3)), jnp.sum(conv * conv, axis=(1, 2,...  38.9 us
    dot_general x27, matrix products, contract(): jnp.einsum('oxyz,ixyz->oi', left, slab, precision=lax.Precision.HIGHEST)  22.7 us
    ppermute x6, waiting for transfers between devices, with_halo(): lax.ppermute(lax.slice_in_dim(block, block.shape[dim] - width, None, axis...  7.88 us
    ppermute x6, starting transfers between devices, with_halo(): lax.ppermute(lax.slice_in_dim(block, block.shape[dim] - width, None, axis...  7.03 us
    ppermute x6, starting transfers between devices, with_halo(): lax.ppermute(lax.slice_in_dim(block, 0, width, axis=dim), axis, backward)  6.81 us
  transfers between devices with their start and end apart: 12, of which 5 were waited for; matrix products, arithmetic and copies ran while one was open for 14% of the time, Pallas kernels for 0%

commit v1 on v0

--- a/solution.py
+++ b/solution.py
@@ -76,8 +76,11 @@
         for second in range(3):
             for third in range(3):
                 pieces.append(contract(conv_grad, window(padded, first, second, third)))
-    weight_grad = lax.psum(
-        jnp.stack(pieces, axis=2).reshape(chans, chans, 3, 3, 3), ("gx", "gy", "gz")
+    weight_grad = jnp.sum(
+        lax.all_gather(
+            jnp.stack(pieces, axis=2).reshape(chans, chans, 3, 3, 3), ("gx", "gy", "gz")
+        ),
+        axis=0,
     )
     grad_padded = with_halo(conv_grad, (("gx", 1), ("gy", 2), ("gz", 3)), 1)
     input_grad = jnp.zeros(volume.shape, jnp.float32)

time: 255 us -> 307 us (1.20)
  blocking collectives: 121 us -> 175 us
  waiting for transfers between devices: 10.9 us -> 6.18 us
  other arithmetic: 7.77 us -> 12 us
    all_gather x0 -> x1, blocking collectives: none -> 96.1 us  [shards(): lax.all_gather(jnp.stack(pieces, axis=2).reshape(chans, chans, 3, 3, 3),...]
    psum x1 -> x0, blocking collectives: 41.9 us -> none  [shards(): lax.psum(jnp.stack(pieces, axis=2).reshape(chans, chans, 3, 3, 3), ('gx',...]
    ppermute x6, waiting for transfers between devices: 7.88 us -> 2.88 us  [with_halo(): lax.ppermute(lax.slice_in_dim(block, block.shape[dim] - width, None, axis...]
    reduce_sum x0 -> x1, other arithmetic: none -> 4.19 us  [shards(): jnp.sum(lax.all_gather(jnp.stack(pieces, axis=2).reshape(chans, chans, 3,...]
  transfers between devices with their start and end apart: 12 -> 12, of which waited for: 5 -> 5; matrix products, arithmetic and copies ran while one was open for 14% -> 13% of each run, Pallas kernels for 0% -> 0%
where the time goes in v1:
time: 307 us; the launch traced here: 303 us
  blocking collectives  175 us (57%)
  matrix products  78.8 us (26%)
  local copies, waits for them, and re-layouts  15 us (5%)
  starting transfers between devices  13.7 us (4%)
  other arithmetic  12 us (4%)
  waiting for transfers between devices  6.18 us (2%)
    all_gather x1, blocking collectives, shards(): lax.all_gather(jnp.stack(pieces, axis=2).reshape(chans, chans, 3, 3, 3),...  96.1 us
    dot_general x54, matrix products, mix(): jnp.einsum('oi,ixyz->oxyz', kernel, slab, precision=lax.Precision.HIGHEST)  56.1 us
    psum x1, blocking collectives, shards(): lax.psum((jnp.sum(act_grad * normed, axis=(1, 2, 3)), jnp.sum(act_grad, a...  40.5 us
    psum x1, blocking collectives, shards(): lax.psum((jnp.sum(conv, axis=(1, 2, 3)), jnp.sum(conv * conv, axis=(1, 2,...  38.9 us
    dot_general x27, matrix products, contract(): jnp.einsum('oxyz,ixyz->oi', left, slab, precision=lax.Precision.HIGHEST)  22.7 us
    ppermute x6, starting transfers between devices, with_halo(): lax.ppermute(lax.slice_in_dim(block, block.shape[dim] - width, None, axis...  7.47 us
    ppermute x6, starting transfers between devices, with_halo(): lax.ppermute(lax.slice_in_dim(block, 0, width, axis=dim), axis, backward)  6.21 us
  transfers between devices with their start and end apart: 12, of which 5 were waited for; matrix products, arithmetic and copies ran while one was open for 13% of the time, Pallas kernels for 0%

profile of v1, /device:TPU:0, one launch (start us, length us, event | category | flops | bytes accessed | tf_op | source)
XLA Modules:
  0.0 302.9 jit_solution(798166474594075779)
XLA Ops:
  0.6 1.1 fusion.319
  1.7 3.0 %collective-permute-start = (f32[16,1,16,128]{3,0,2,1:T(8,128)S(1)}, f32[16,1,16,128]{3,0,2,1:T(8,128)S(1)}, u32[]{:S(2)}, u32[]{:S(2)}) collective-permute-start(f32[16,1,16,128]{3,0,2,1:T(8,128)S(1)} %copy.207), channel_id=1, source_target_pairs={{0,16},{16,0},{1,17},{17,1},{2,18},{18,2},{3,19},{19,3},{4,20},{20... | collective-permute-start | bytes 393224 | tf_op jit(solution)/shard_map/ppermute | solution.py:13
  4.9 2.7 fusion.206
  7.6 1.5 collective-permute-done
  9.5 1.6 collective-permute-done.1
  11.1 1.9 collective-permute-start.2
  13.0 2.1 collective-permute-start.3
  15.1 2.1 fusion.225
  17.2 2.1 convolution_bitcast_fusion.4
  21.0 1.9 collective-permute-start.5
  23.0 2.1 fusion.85
  25.0 2.0 fusion.86
  27.1 2.1 fusion.87
  29.2 2.1 convolution_bitcast_fusion.3
  31.2 2.1 convolution_bitcast_fusion.5
  33.3 2.1 convolution_bitcast_fusion.6
  36.1 1.6 copy.51
  37.7 1.8 maximum_maximum_fusion
  47.1 1.1 convolution_bitcast_fusion.18
  50.2 1.0 fusion.44
  51.6 1.2 fusion.312
  52.8 38.9 %all-reduce.1 = (f32[16]{0:T(128)S(1)}, f32[16]{0:T(128)S(1)}) all-reduce(f32[16]{0:T(128)S(1)} %get-tuple-element.15, f32[16]{0:T(128)S(1)} %get-tuple-element.14), channel_id=1, replica_groups=mesh['gx'=2,'gy'=4,'gz'=4] {'gx','gy','gz'}, use_global_device_ids=true, to_apply=%region_1.0 | all-reduce | flops 32 | bytes 256 | tf_op jit(solution)/shard_map/psum | solution.py:53
  91.7 2.4 fusion.311
  94.1 40.5 %all-reduce = (f32[16]{0:T(128)S(1)}, f32[16]{0:T(128)S(1)}) all-reduce(f32[16]{0:T(128)S(1)} %get-tuple-element.13, f32[16]{0:T(128)S(1)} %get-tuple-element.12), channel_id=1, replica_groups=mesh['gx'=2,'gy'=4,'gz'=4] {'gx','gy','gz'}, use_global_device_ids=true, to_apply=%region_7.0 | all-reduce | flops 32 | bytes 256 | tf_op jit(solution)/shard_map/psum | solution.py:65
  134.6 1.4 subtract_multiply_fusion
  147.5 1.0 fusion.64
  155.1 1.0 fusion.55
  159.5 96.1 %all_gather.3 = f32[32,16,16,3,3,3]{2,1,5,4,3,0:T(8,128)} all-gather(f32[1,16,16,3,3,3]{2,1,5,4,3,0:T(8,128)S(1)} %bitcast.644), channel_id=1, replica_groups=mesh['gx'=2,'gy'=4,'gz'=4] {'gx','gy','gz'}, dimensions={0}, use_global_device_ids=true | all-gather | bytes 912384 | tf_op jit(solution)/shard_map/all_gather | solution.py:80
  255.6 2.0 collective-permute-start.7
  257.6 4.2 %reduce_sum.49 = f32[16,16,3,3,3]{1,0,4,3,2:T(8,128)} reduce(f32[32,16,16,3,3,3]{2,1,5,4,3,0:T(8,128)} %all_gather.3, f32[]{:T(128)} %constant.8.clone.1), dimensions={0}, to_apply=%region_8.0 | reduce | flops 214272 | bytes 912388 | tf_op jit(solution)/shard_map/reduce_sum | solution.py:79
  261.8 1.4 fusion.204
  263.2 1.2 collective-permute-done.7
  264.5 2.0 collective-permute-start.8
  266.5 1.4 fusion.78
  269.1 1.3 collective-permute-done.8
  270.5 1.2 fusion.315
  271.7 1.8 copy.56
  274.8 1.4 fusion.177
  276.2 1.4 fusion.175
  277.6 1.4 fusion.176
  279.0 1.4 fusion.174
  280.4 1.4 convolution_bitcast_fusion.2
  281.8 1.4 convolution_bitcast_fusion
  283.2 1.6 copy.57
  284.8 1.6 copy.61
  286.4 2.0 pad_maximum_fusion.3
  299.4 1.1 fusion.46
  300.7 1.0 fusion.48
  (153 shorter events, 48.5 us)
Async XLA Ops:
  0.6 8.5 %copy-start.2 = (f32[16,4,16,128]{3,2,1,0:T(8,128)S(1)}, f32[16,4,16,128]{3,2,1,0:T(8,128)}, u32[]{:S(2)}) copy-start(f32[16,4,16,128]{3,2,1,0:T(8,128)} %param.5) | copy-start | bytes 1572868
  1.7 7.4 %collective-permute-start = (f32[16,1,16,128]{3,0,2,1:T(8,128)S(1)}, f32[16,1,16,128]{3,0,2,1:T(8,128)S(1)}, u32[]{:S(2)}, u32[]{:S(2)}) collective-permute-start(f32[16,1,16,128]{3,0,2,1:T(8,128)S(1)} %copy.207), channel_id=1, source_target_pairs={{0,16},{16,0},{1,17},{17,1},{2,18},{18,2},{3,19},{19,3},{4,20},{20... | collective-permute-start | bytes 393224 | tf_op jit(solution)/shard_map/ppermute | solution.py:13
  4.8 6.3 %collective-permute-start.1 = (f32[16,1,16,128]{3,0,2,1:T(8,128)S(1)}, f32[16,1,16,128]{3,0,2,1:T(8,128)S(1)}, u32[]{:S(2)}, u32[]{:S(2)}) collective-permute-start(f32[16,1,16,128]{3,0,2,1:T(8,128)S(1)} %copy.208), channel_id=1, source_target_pairs={{16,0},{0,16},{17,1},{1,17},{18,2},{2,18},{19,3},{3,19},{20,4},{4,... | collective-permute-start | bytes 393224 | tf_op jit(solution)/shard_map/ppermute | solution.py:16
  9.5 9.8 %copy-start.7 = (f32[16,5,16,128]{3,0,2,1:T(8,128)}, f32[16,5,16,128]{3,0,2,1:T(8,128)S(1)}, u32[]{:S(2)}) copy-start(f32[16,5,16,128]{3,0,2,1:T(8,128)S(1)} %get-tuple-element.37) | copy-start | bytes 1966084
  11.1 8.1 %copy-start.5 = (f32[16,5,16,128]{3,0,2,1:T(8,128)}, f32[16,5,16,128]{3,0,2,1:T(8,128)S(1)}, u32[]{:S(2)}) copy-start(f32[16,5,16,128]{3,0,2,1:T(8,128)S(1)} %get-tuple-element.44) | copy-start | bytes 1966084
  11.1 8.1 %collective-permute-start.2 = (f32[16,6,1,128]{3,0,2,1:T(8,128)S(1)}, f32[16,6,1,128]{3,0,2,1:T(8,128)S(1)}, u32[]{:S(2)}, u32[]{:S(2)}) collective-permute-start(f32[16,6,1,128]{3,0,2,1:T(8,128)S(1)} %get-tuple-element.33), channel_id=1, source_target_pairs={{0,4},{4,8},{8,12},{12,0},{1,5},{5,9},{9,13},{13,1},{2,6},{6,10},{... | collective-permute-start | bytes 147464 | tf_op jit(solution)/shard_map/ppermute | solution.py:13
  13.0 6.2 %collective-permute-start.3 = (f32[16,6,1,128]{3,0,2,1:T(8,128)S(1)}, f32[16,6,1,128]{3,0,2,1:T(8,128)S(1)}, u32[]{:S(2)}, u32[]{:S(2)}) collective-permute-start(f32[16,6,1,128]{3,0,2,1:T(8,128)S(1)} %get-tuple-element.34), channel_id=1, source_target_pairs={{4,0},{8,4},{12,8},{0,12},{5,1},{9,5},{13,9},{1,13},{6,2},{10,6},{... | collective-permute-start | bytes 147464 | tf_op jit(solution)/shard_map/ppermute | solution.py:16
  20.3 15.1 %collective-permute-start.4 = (f32[16,6,18,1]{2,0,3,1:T(8,128)S(1)}, f32[16,6,18,1]{2,0,3,1:T(8,128)S(1)}, u32[]{:S(2)}, u32[]{:S(2)}) collective-permute-start(f32[16,6,18,1]{2,0,3,1:T(8,128)S(1)} %copy.48), channel_id=1, source_target_pairs={{0,1},{1,2},{2,3},{3,0},{4,5},{5,6},{6,7},{7,4},{8,9},{9,10},{10,1... | collective-permute-start | bytes 20744 | tf_op jit(solution)/shard_map/ppermute | solution.py:13
  21.0 15.1 %collective-permute-start.5 = (f32[16,6,18,1]{2,0,3,1:T(8,128)S(1)}, f32[16,6,18,1]{2,0,3,1:T(8,128)S(1)}, u32[]{:S(2)}, u32[]{:S(2)}) collective-permute-start(f32[16,6,18,1]{2,0,3,1:T(8,128)S(1)} %copy.50), channel_id=1, source_target_pairs={{1,0},{2,1},{3,2},{0,3},{5,4},{6,5},{7,6},{4,7},{9,8},{10,9},{11,1... | collective-permute-start | bytes 20744 | tf_op jit(solution)/shard_map/ppermute | solution.py:16
  37.7 1.8 copy-start.26
  39.5 11.6 %copy-start = (f32[16,6,18,129]{3,0,2,1:T(8,128)}, f32[16,6,18,129]{3,0,2,1:T(8,128)S(1)}, u32[]{:S(2)}) copy-start(f32[16,6,18,129]{3,0,2,1:T(8,128)S(1)} %get-tuple-element.28) | copy-start | bytes 2674948
  48.2 1.9 copy-start.11
  48.2 1.9 copy-start.12
  48.2 1.9 copy-start.23
  48.2 1.9 copy-start.24
  48.2 1.9 copy-start.25
  50.1 1.0 copy-start.9
  50.1 1.2 copy-start.17
  50.1 1.3 copy-start.18
  50.2 1.5 copy-start.19
  51.6 40.1 %copy-start.28 = (f32[16]{0:T(128)S(1)}, f32[16]{0:T(128)}, u32[]{:S(2)}) copy-start(f32[16]{0:T(128)} %param.7) | copy-start | bytes 196
  51.6 40.1 %copy-start.29 = (f32[16]{0:T(128)S(1)}, f32[16]{0:T(128)}, u32[]{:S(2)}) copy-start(f32[16]{0:T(128)} %param.8) | copy-start | bytes 196
  52.8 81.8 %copy-start.4 = (f32[16,4,16,128]{3,0,2,1:T(8,128)}, f32[16,4,16,128]{3,0,2,1:T(8,128)S(1)}, u32[]{:S(2)}) copy-start(f32[16,4,16,128]{3,0,2,1:T(8,128)S(1)} %get-tuple-element.47) | copy-start | bytes 1572868
  134.6 3.7 %copy-start.30 = (f32[16]{0:T(128)}, f32[16]{0:T(128)S(1)}, u32[]{:S(2)}) copy-start(f32[16]{0:T(128)S(1)} %get-tuple-element.16) | copy-start | bytes 196
  134.6 3.7 %copy-start.31 = (f32[16]{0:T(128)}, f32[16]{0:T(128)S(1)}, u32[]{:S(2)}) copy-start(f32[16]{0:T(128)S(1)} %get-tuple-element.17) | copy-start | bytes 196
  136.0 2.3 copy-start.1
  137.5 2.5 copy-start.8
  145.0 2.5 copy-start.3
  152.7 2.5 copy-start.6
  255.6 7.6 %collective-permute-start.6 = (f32[16,1,16,128]{3,0,2,1:T(8,128)}, f32[16,1,16,128]{3,0,2,1:T(8,128)S(1)}, u32[]{:S(2)}, u32[]{:S(2)}) collective-permute-start(f32[16,1,16,128]{3,0,2,1:T(8,128)} %get-tuple-element.35), channel_id=1, source_target_pairs={{0,16},{16,0},{1,17},{17,1},{2,18},{18,2},{3,19},{19,3},{4,20},{20... | collective-permute-start | bytes 393224 | tf_op jit(solution)/shard_map/ppermute | solution.py:13
  255.6 6.2 %copy-start.27 = (f32[16,16,3,3,3]{1,0,4,3,2:T(8,128)S(1)}, f32[16,16,3,3,3]{1,0,4,3,2:T(8,128)}, u32[]{:S(2)}) copy-start(f32[16,16,3,3,3]{1,0,4,3,2:T(8,128)} %param.6) | copy-start | bytes 82948
  255.6 8.8 %collective-permute-start.7 = (f32[16,1,16,128]{3,0,2,1:T(8,128)}, f32[16,1,16,128]{3,0,2,1:T(8,128)S(1)}, u32[]{:S(2)}, u32[]{:S(2)}) collective-permute-start(f32[16,1,16,128]{3,0,2,1:T(8,128)} %get-tuple-element.36), channel_id=1, source_target_pairs={{16,0},{0,16},{17,1},{1,17},{18,2},{2,18},{19,3},{3,19},{20,4},{4,... | collective-permute-start | bytes 393224 | tf_op jit(solution)/shard_map/ppermute | solution.py:16
  264.4 4.7 %collective-permute-start.9 = (f32[16,6,1,128]{3,0,2,1:T(8,128)S(1)}, f32[16,6,1,128]{3,0,2,1:T(8,128)S(1)}, u32[]{:S(2)}, u32[]{:S(2)}) collective-permute-start(f32[16,6,1,128]{3,0,2,1:T(8,128)S(1)} %get-tuple-element.32), channel_id=1, source_target_pairs={{4,0},{8,4},{12,8},{0,12},{5,1},{9,5},{13,9},{1,13},{6,2},{10,6},{... | collective-permute-start | bytes 147464 | tf_op jit(solution)/shard_map/ppermute | solution.py:16
  264.5 5.9 %collective-permute-start.8 = (f32[16,6,1,128]{3,0,2,1:T(8,128)S(1)}, f32[16,6,1,128]{3,0,2,1:T(8,128)S(1)}, u32[]{:S(2)}, u32[]{:S(2)}) collective-permute-start(f32[16,6,1,128]{3,0,2,1:T(8,128)S(1)} %get-tuple-element.31), channel_id=1, source_target_pairs={{0,4},{4,8},{8,12},{12,0},{1,5},{5,9},{9,13},{13,1},{2,6},{6,10},{... | collective-permute-start | bytes 147464 | tf_op jit(solution)/shard_map/ppermute | solution.py:13
  273.5 9.7 %collective-permute-start.10 = (f32[16,6,18,1]{2,0,3,1:T(8,128)S(1)}, f32[16,6,18,1]{2,0,3,1:T(8,128)S(1)}, u32[]{:S(2)}, u32[]{:S(2)}) collective-permute-start(f32[16,6,18,1]{2,0,3,1:T(8,128)S(1)} %copy.56), channel_id=1, source_target_pairs={{1,0},{2,1},{3,2},{0,3},{5,4},{6,5},{7,6},{4,7},{9,8},{10,9},{11,1... | collective-permute-start | bytes 20744 | tf_op jit(solution)/shard_map/ppermute | solution.py:16
  274.2 10.6 %collective-permute-start.11 = (f32[16,6,18,1]{2,0,3,1:T(8,128)S(1)}, f32[16,6,18,1]{2,0,3,1:T(8,128)S(1)}, u32[]{:S(2)}, u32[]{:S(2)}) collective-permute-start(f32[16,6,18,1]{2,0,3,1:T(8,128)S(1)} %copy.60), channel_id=1, source_target_pairs={{0,1},{1,2},{2,3},{3,0},{4,5},{5,6},{6,7},{7,4},{8,9},{9,10},{10,1... | collective-permute-start | bytes 20744 | tf_op jit(solution)/shard_map/ppermute | solution.py:13
  297.0 2.3 copy-start.10
  297.0 2.3 copy-start.13
  297.0 2.3 copy-start.20
  297.3 2.1 copy-start.21
  297.3 2.1 copy-start.22
  299.3 1.1 copy-start.14
  299.4 1.2 copy-start.15
  299.4 1.3 copy-start.16
